TPU v7x, 32 devices: a whole 2x2x4 slice. The times are simulated.
32 devices in a mesh: grp: 4 (over z), dev: 8 (over y, x, core).
Axes of the slice: x: 2, y: 2, z: 4, core: 2. Of those that a mesh axis runs over, the one named last changes fastest.
Arguments:
- matrix: float32 [65536, 1024], P(('grp', 'dev')), may hold values from -60 to 60
- block_order: int32 [4, 128], P('grp'), may hold values from 0 to 127, as said below
- counts: int32 [4, 8], P('grp'), may hold values from 0 to 32, as said below
- sign_bits: int32 [4, 128, 128], P('grp'), may hold values from 0 to 1
- row_mask: int32 [4, 128, 128], P('grp'), may hold values from 0 to 1, as said below
Outputs:
- sketch: float32 [32768, 1024], P(('grp', 'dev'))
- group_factor: float32 [4, 1024, 1024], P('grp', 'dev')
- factor: float32 [1024, 1024], P('dev')
Inputs may be any that keep to these rules, and one draw needn't show every extreme that they name: Each row of block_order is a permutation of the group's block indices; at most 4 blocks of one device's blocks are placed in the positions held by one device, and some pair reaches 4. `counts`: each row sums to 128; its largest entry is exactly 32. `row_mask`: exactly 32 ones in each row of 128.
All inputs are finite; a program needn't handle non-finite values.
Results may differ from a plain program's by a relative error of at most 0.0003.
Values sent between devices are 32-bit elements; how exact they have to be, the bound alone decides.
No kernel may reach another device: no remote copies, remote signals or barrier semaphores. Data moves between devices by JAX's collectives and lax.ppermute only.
A program may use at most 128 MiB of HBM per device.

v0:
```python
import jax
import jax.numpy as jnp
from jax import lax
from jax.sharding import PartitionSpec as P

BLOCK = 128
KEEP = 32


def hadamard(order_of):
    indices = jnp.arange(order_of, dtype=jnp.int32)
    common = jnp.bitwise_and(indices[:, None], indices[None, :])
    parity = jnp.zeros_like(common)
    for shift_by in range(order_of.bit_length() - 1):
        parity = parity + jnp.bitwise_and(jnp.right_shift(common, shift_by), 1)
    return (1 - 2 * (parity % 2)).astype(jnp.float32)


def mix_blocks(block_list, mask_rows, sign_rows, walsh_sign_matrix):
    running = jnp.cumsum(mask_rows, axis=1) - 1
    choose_row = jnp.arange(KEEP, dtype=jnp.int32)[None, :, None]
    select_rows = ((mask_rows[:, None, :] == 1) & (running[:, None, :] == choose_row)).astype(
        jnp.float32
    )
    mixing_transform = jnp.einsum(
        "jlf,fp->jlp", select_rows, walsh_sign_matrix, precision=lax.Precision.HIGHEST
    )
    mixing_transform = mixing_transform * (1 - 2 * sign_rows).astype(jnp.float32)[:, None, :]
    normalize_rows = float(walsh_sign_matrix.shape[0]) ** (-0.5)
    return (
        jnp.einsum("uwd,udk->uwk", mixing_transform, block_list, precision=lax.Precision.HIGHEST)
        * normalize_rows
    )


def gram_of(mixed_rows):
    flat_rows = mixed_rows.reshape(-1, mixed_rows.shape[-1])
    return jnp.einsum("kc,ke->ce", flat_rows, flat_rows, precision=lax.Precision.HIGHEST)


def body(matrix, block_order, counts, sign_bits, row_mask):
    blocks_dev = matrix.shape[0] // BLOCK
    columns = matrix.shape[1]
    devices = lax.axis_size("dev")
    groups = lax.axis_size("grp")
    me_dev = lax.axis_index("dev")
    positions = devices * blocks_dev
    most_held = 2 * blocks_dev
    capacity = max(1, 2 * blocks_dev // devices)
    order_row = block_order[0]
    count_row = counts[0]
    sign_table = sign_bits[0]
    mask_table = row_mask[0]
    run_ends = jnp.cumsum(count_row)
    offsets = run_ends - count_row
    block_locations = jnp.arange(positions, dtype=jnp.int32)
    owners = jnp.sum((block_locations[:, None] >= run_ends[None, :]).astype(jnp.int32), axis=1)
    source = order_row // blocks_dev
    earlier = (
        (block_locations[None, :] < block_locations[:, None])
        & (owners[None, :] == owners[:, None])
        & (source[None, :] == source[:, None])
    )
    slot_of = jnp.sum(earlier.astype(jnp.int32), axis=1)
    target = owners * capacity + slot_of
    inverse = jnp.zeros((positions,), jnp.int32).at[order_row].set(block_locations)
    my_places = lax.dynamic_slice_in_dim(inverse, me_dev * blocks_dev, blocks_dev)
    my_target = target[my_places]
    buffer_slots = jnp.arange(devices * capacity, dtype=jnp.int32)
    matches = my_target[None, :] == buffer_slots[:, None]
    filled = jnp.any(matches, axis=1)
    pick_block = jnp.sum(
        matches.astype(jnp.int32) * jnp.arange(blocks_dev, dtype=jnp.int32)[None, :], axis=1
    )
    held_slots = jnp.arange(most_held, dtype=jnp.int32)
    my_count = lax.dynamic_index_in_dim(count_row, me_dev, 0, False)
    my_offset = lax.dynamic_index_in_dim(offsets, me_dev, 0, False)
    live_slot = held_slots < my_count
    my_positions = jnp.minimum(my_offset + held_slots, positions - 1)
    from_slot = source[my_positions] * capacity + slot_of[my_positions]
    local_blocks = matrix.reshape(blocks_dev, BLOCK, columns)
    walsh_sign_matrix = hadamard(BLOCK)
    mixed_rows = mix_blocks(
        local_blocks, mask_table[my_places], sign_table[my_places], walsh_sign_matrix
    )
    partial_value = gram_of(mixed_rows)
    outgoing = jnp.where(filled[:, None, None], jnp.take(mixed_rows, pick_block, axis=0), 0.0)
    arrived = lax.all_to_all(outgoing, "dev", split_axis=0, concat_axis=0, tiled=True)
    sketch = jnp.where(live_slot[:, None, None], jnp.take(arrived, from_slot, axis=0), 0.0)
    group_gram = lax.psum(partial_value, "dev") / float(positions * KEEP)
    mean_gram = lax.psum(group_gram, "grp") / float(groups)
    rows_dev = columns // devices
    group_upper = jnp.linalg.cholesky(group_gram).T
    mean_upper = jnp.linalg.cholesky(mean_gram).T
    group_factor = lax.dynamic_slice_in_dim(group_upper, me_dev * rows_dev, rows_dev, 0)[None]
    factor = lax.dynamic_slice_in_dim(mean_upper, me_dev * rows_dev, rows_dev, 0)
    return (sketch.reshape(most_held * KEEP, columns), group_factor, factor)


def solution(mesh):
    placed = (
        P(("grp", "dev"), None),
        P("grp", None),
        P("grp", None),
        P("grp", None, None),
        P("grp", None, None),
    )
    return jax.shard_map(
        body,
        mesh=mesh,
        in_specs=placed,
        out_specs=(P(("grp", "dev"), None), P("grp", "dev", None), P("dev", None)),
        check_vma=False,
    )
```

profile of v0, /device:TPU:26, one launch (start us, length us, event | category | flops | bytes accessed | tf_op | source)
XLA Modules:
  0.0 601.2 jit_solution(12430598933679036047)
XLA Ops:
  18.4 8.4 %convolution_bitcast_fusion = f32[1024,1024]{0,1:T(8,128)} fusion(f32[16,32,1024]{2,1,0:T(8,128)S(1)} %convolution_multiply_fusion), kind=kOutput, calls=%fused_computation.16 | convolution fusion | flops 6442450944 | bytes 6291456 | tf_op jit(solution)/shard_map/kc,ke->ce/dot_general | solution.py:38
  46.5 92.8 %all-reduce.4.cloned.1.call-done = f32[1024,1024]{0,1:T(8,128)} async-done(((f32[1024,1024]{0,1:T(8,128)}), f32[1024,1024]{0,1:T(8,128)}) %all-reduce.4.cloned.1.call-update) | async-done | bytes 4194320 | tf_op jit(solution)/shard_map/psum | solution.py:90
  156.9 11.7 %cholesky.619 = f32[128,128]{1,0:T(8,128)S(1)} custom-call(f32[128,128]{1,0:T(8,128)S(1)} %cholesky.911), custom_call_target="Cholesky" | custom-call | tf_op jit(solution)/shard_map/jit(cholesky)/cholesky | solution.py:93
  168.7 9.8 %custom-call.51 = f32[1,128,128]{1,2,0:T(8,128)S(1)} custom-call(f32[1,128,128]{2,1,0:T(8,128)S(1)} %get-tuple-element.58), custom_call_target="InvertDiagBlocksLowerTriangular" | custom-call | tf_op jit(solution)/shard_map/jit(cholesky)/cholesky | solution.py:93
  184.8 11.9 %cholesky.638 = f32[128,128]{1,0:T(8,128)S(1)} custom-call(f32[128,128]{1,0:T(8,128)S(1)} %cholesky.915), custom_call_target="Cholesky" | custom-call | tf_op jit(solution)/shard_map/jit(cholesky)/cholesky | solution.py:93
  197.4 9.8 %custom-call.52 = f32[1,128,128]{1,2,0:T(8,128)S(1)} custom-call(f32[1,128,128]{2,1,0:T(8,128)S(1)} %get-tuple-element.55), custom_call_target="InvertDiagBlocksLowerTriangular" | custom-call | tf_op jit(solution)/shard_map/jit(cholesky)/cholesky | solution.py:93
  210.5 11.7 %cholesky.659 = f32[128,128]{1,0:T(8,128)S(1)} custom-call(f32[128,128]{1,0:T(8,128)S(1)} %cholesky.920), custom_call_target="Cholesky" | custom-call | tf_op jit(solution)/shard_map/jit(cholesky)/cholesky | solution.py:93
  222.9 9.8 %custom-call.53 = f32[1,128,128]{1,2,0:T(8,128)S(1)} custom-call(f32[1,128,128]{2,1,0:T(8,128)S(1)} %get-tuple-element.52), custom_call_target="InvertDiagBlocksLowerTriangular" | custom-call | tf_op jit(solution)/shard_map/jit(cholesky)/cholesky | solution.py:93
  236.3 11.9 %cholesky.678 = f32[128,128]{1,0:T(8,128)S(1)} custom-call(f32[128,128]{1,0:T(8,128)S(1)} %cholesky.925), custom_call_target="Cholesky" | custom-call | tf_op jit(solution)/shard_map/jit(cholesky)/cholesky | solution.py:93
  248.8 9.8 %custom-call.54 = f32[1,128,128]{1,2,0:T(8,128)S(1)} custom-call(f32[1,128,128]{2,1,0:T(8,128)S(1)} %get-tuple-element.49), custom_call_target="InvertDiagBlocksLowerTriangular" | custom-call | tf_op jit(solution)/shard_map/jit(cholesky)/cholesky | solution.py:93
  262.1 11.7 %cholesky.697 = f32[128,128]{1,0:T(8,128)S(1)} custom-call(f32[128,128]{1,0:T(8,128)S(1)} %cholesky.930), custom_call_target="Cholesky" | custom-call | tf_op jit(solution)/shard_map/jit(cholesky)/cholesky | solution.py:93
  274.5 10.2 %custom-call.55 = f32[1,128,128]{1,2,0:T(8,128)S(1)} custom-call(f32[1,128,128]{2,1,0:T(8,128)S(1)} %get-tuple-element.46), custom_call_target="InvertDiagBlocksLowerTriangular" | custom-call | tf_op jit(solution)/shard_map/jit(cholesky)/cholesky | solution.py:93
  287.9 11.7 %cholesky.716 = f32[128,128]{1,0:T(8,128)S(1)} custom-call(f32[128,128]{1,0:T(8,128)S(1)} %cholesky.935), custom_call_target="Cholesky" | custom-call | tf_op jit(solution)/shard_map/jit(cholesky)/cholesky | solution.py:93
  300.3 9.8 %custom-call.56 = f32[1,128,128]{1,2,0:T(8,128)S(1)} custom-call(f32[1,128,128]{2,1,0:T(8,128)S(1)} %get-tuple-element.43), custom_call_target="InvertDiagBlocksLowerTriangular" | custom-call | tf_op jit(solution)/shard_map/jit(cholesky)/cholesky | solution.py:93
  313.2 11.9 %cholesky.735 = f32[128,128]{1,0:T(8,128)S(1)} custom-call(f32[128,128]{1,0:T(8,128)S(1)} %cholesky.940), custom_call_target="Cholesky" | custom-call | tf_op jit(solution)/shard_map/jit(cholesky)/cholesky | solution.py:93
  325.7 9.8 %custom-call.57 = f32[1,128,128]{1,2,0:T(8,128)S(1)} custom-call(f32[1,128,128]{2,1,0:T(8,128)S(1)} %get-tuple-element.40), custom_call_target="InvertDiagBlocksLowerTriangular" | custom-call | tf_op jit(solution)/shard_map/jit(cholesky)/cholesky | solution.py:93
  338.1 11.7 %cholesky.752 = f32[128,128]{1,0:T(8,128)S(1)} custom-call(f32[128,128]{1,0:T(8,128)S(1)} %convolution_subtract_fusion.13), custom_call_target="Cholesky" | custom-call | tf_op jit(solution)/shard_map/jit(cholesky)/cholesky | solution.py:93
  386.9 11.7 %cholesky.767 = f32[128,128]{1,0:T(8,128)S(1)} custom-call(f32[128,128]{1,0:T(8,128)S(1)} %cholesky.945), custom_call_target="Cholesky" | custom-call | tf_op jit(solution)/shard_map/jit(cholesky)/cholesky | solution.py:94
  401.1 9.8 %custom-call.58 = f32[1,128,128]{1,2,0:T(8,128)S(1)} custom-call(f32[1,128,128]{2,1,0:T(8,128)S(1)} %get-tuple-element.36), custom_call_target="InvertDiagBlocksLowerTriangular" | custom-call | tf_op jit(solution)/shard_map/jit(cholesky)/cholesky | solution.py:94
  414.9 12.1 %cholesky.786 = f32[128,128]{1,0:T(8,128)S(1)} custom-call(f32[128,128]{1,0:T(8,128)S(1)} %cholesky.949), custom_call_target="Cholesky" | custom-call | tf_op jit(solution)/shard_map/jit(cholesky)/cholesky | solution.py:94
  428.9 9.8 %custom-call.59 = f32[1,128,128]{1,2,0:T(8,128)S(1)} custom-call(f32[1,128,128]{2,1,0:T(8,128)S(1)} %get-tuple-element.33), custom_call_target="InvertDiagBlocksLowerTriangular" | custom-call | tf_op jit(solution)/shard_map/jit(cholesky)/cholesky | solution.py:94
  442.0 11.7 %cholesky.807 = f32[128,128]{1,0:T(8,128)S(1)} custom-call(f32[128,128]{1,0:T(8,128)S(1)} %cholesky.954), custom_call_target="Cholesky" | custom-call | tf_op jit(solution)/shard_map/jit(cholesky)/cholesky | solution.py:94
  455.0 9.8 %custom-call.60 = f32[1,128,128]{1,2,0:T(8,128)S(1)} custom-call(f32[1,128,128]{2,1,0:T(8,128)S(1)} %get-tuple-element.30), custom_call_target="InvertDiagBlocksLowerTriangular" | custom-call | tf_op jit(solution)/shard_map/jit(cholesky)/cholesky | solution.py:94
  468.3 11.9 %cholesky.826 = f32[128,128]{1,0:T(8,128)S(1)} custom-call(f32[128,128]{1,0:T(8,128)S(1)} %cholesky.959), custom_call_target="Cholesky" | custom-call | tf_op jit(solution)/shard_map/jit(cholesky)/cholesky | solution.py:94
  481.5 9.8 %custom-call.61 = f32[1,128,128]{1,2,0:T(8,128)S(1)} custom-call(f32[1,128,128]{2,1,0:T(8,128)S(1)} %get-tuple-element.27), custom_call_target="InvertDiagBlocksLowerTriangular" | custom-call | tf_op jit(solution)/shard_map/jit(cholesky)/cholesky | solution.py:94
  494.8 11.7 %cholesky.845 = f32[128,128]{1,0:T(8,128)S(1)} custom-call(f32[128,128]{1,0:T(8,128)S(1)} %cholesky.964), custom_call_target="Cholesky" | custom-call | tf_op jit(solution)/shard_map/jit(cholesky)/cholesky | solution.py:94
  507.8 10.0 %custom-call.62 = f32[1,128,128]{1,2,0:T(8,128)S(1)} custom-call(f32[1,128,128]{2,1,0:T(8,128)S(1)} %get-tuple-element.24), custom_call_target="InvertDiagBlocksLowerTriangular" | custom-call | tf_op jit(solution)/shard_map/jit(cholesky)/cholesky | solution.py:94
  521.1 11.7 %cholesky.864 = f32[128,128]{1,0:T(8,128)S(1)} custom-call(f32[128,128]{1,0:T(8,128)S(1)} %cholesky.969), custom_call_target="Cholesky" | custom-call | tf_op jit(solution)/shard_map/jit(cholesky)/cholesky | solution.py:94
  534.1 9.8 %custom-call.63 = f32[1,128,128]{1,2,0:T(8,128)S(1)} custom-call(f32[1,128,128]{2,1,0:T(8,128)S(1)} %get-tuple-element.21), custom_call_target="InvertDiagBlocksLowerTriangular" | custom-call | tf_op jit(solution)/shard_map/jit(cholesky)/cholesky | solution.py:94
  546.9 11.9 %cholesky.883 = f32[128,128]{1,0:T(8,128)S(1)} custom-call(f32[128,128]{1,0:T(8,128)S(1)} %cholesky.974), custom_call_target="Cholesky" | custom-call | tf_op jit(solution)/shard_map/jit(cholesky)/cholesky | solution.py:94
  560.1 9.8 %custom-call.64 = f32[1,128,128]{1,2,0:T(8,128)S(1)} custom-call(f32[1,128,128]{2,1,0:T(8,128)S(1)} %get-tuple-element.18), custom_call_target="InvertDiagBlocksLowerTriangular" | custom-call | tf_op jit(solution)/shard_map/jit(cholesky)/cholesky | solution.py:94
  572.6 11.7 %cholesky.900 = f32[128,128]{1,0:T(8,128)S(1)} custom-call(f32[128,128]{1,0:T(8,128)S(1)} %convolution_subtract_fusion.12), custom_call_target="Cholesky" | custom-call | tf_op jit(solution)/shard_map/jit(cholesky)/cholesky | solution.py:94
  (147 shorter events, 148.4 us)
Async XLA Ops:
  7.2 1.8 copy-start
  7.2 132.2 %all-reduce.4.cloned.1.call-start = ((), (), s32[]{:S(2)}) async-start(), calls=%async_computation.1 | async-start | bytes 8388608 | tf_op jit(solution)/shard_map/psum | solution.py:90
  26.7 0.7 copy-start.4
  26.7 0.7 copy-start.5
  39.7 321.1 %all-to-all-start = ((f32[32,32,1024]{2,1,0:T(8,128)}), f32[32,32,1024]{2,1,0:T(8,128)}, u32[]{:S(2)}, u32[]{:S(2)}) async-start(f32[32,32,1024]{2,1,0:T(8,128)} %select_select_fusion), calls=%async_computation | async-start | bytes 8388608 | tf_op jit(solution)/shard_map/all_to_all | solution.py:88
  149.8 220.2 %all-reduce.6.cloned.1.call-start = ((), (), s32[]{:S(2)}) async-start(), calls=%async_computation.2 | async-start | bytes 8388608 | tf_op jit(solution)/shard_map/psum | solution.py:91
  154.9 2.0 copy-start.3
  384.9 1.9 copy-start.2
  518.8 75.1 %copy-start.1 = (s32[1,128,128]{2,1,0:T(8,128)S(1)}, s32[1,128,128]{2,1,0:T(8,128)}, u32[]{:S(2)}) copy-start(s32[1,128,128]{2,1,0:T(8,128)} %param.10) | copy-start | bytes 196612
Sparse Core Ops, SparseCore 0:
  26.9 112.4 all-reduce.3
  152.9 153.1 all-reduce.5
where the time goes:
time: 611 us; the launch traced here: 601 us
  other arithmetic  379 us (62%)
  waiting for transfers between devices  93.1 us (15%)
  matrix products  61.8 us (10%)
  local copies, waits for them, and re-layouts  36.9 us (6%)
  between operations  25.1 us (4%)
    another operation x31, other arithmetic, body(): mean_upper = jnp.linalg.cholesky(mean_gram).T  173 us
    another operation x31, other arithmetic, body(): group_upper = jnp.linalg.cholesky(group_gram).T  173 us
    psum x1, waiting for transfers between devices, body(): group_gram = lax.psum(partial_value, 'dev') / float(positions * KEEP)  92.8 us
    another operation x14, matrix products, body(): group_upper = jnp.linalg.cholesky(group_gram).T  23.2 us
    another operation x14, matrix products, body(): mean_upper = jnp.linalg.cholesky(mean_gram).T  23.1 us
  transfers between devices with their start and end apart: 3, of which 1 were waited for; matrix products, arithmetic and copies ran while one was open for 39% of the time, Pallas kernels for 0%

commit v1 on v0

v1 whole, which is shorter than its diff:
```python
import jax
import jax.numpy as jnp
from jax import lax
from jax.experimental import pallas as pl
from jax.experimental.pallas import tpu as pltpu
from jax.sharding import PartitionSpec as P

BLOCK = 128
KEEP = 32
PB = 128
BS = 16
STEP = 2
f32 = jnp.float32
bf16 = jnp.bfloat16


def split(x):
    high = x.astype(bf16)
    return high, (x - high.astype(f32)).astype(bf16)


def dg(a, b, ca=1, cb=0):
    return lax.dot_general(a, b, (((ca,), (cb,)), ((), ())), preferred_element_type=f32)


def dot3(a, b, ca=1, cb=0):
    return dg(a[0], b[0], ca, cb) + (dg(a[0], b[1], ca, cb) + dg(a[1], b[0], ca, cb))


def iota(shape, axis):
    return lax.broadcasted_iota(jnp.int32, shape, axis)


def mix_kernel(blocks_dev, devices, capacity, scale):
    def kernel(me_ref, order_ref, counts_ref, sign_ref, mask_ref, x_ref, slots_ref, gram_ref,
               places, targets, filled, transform, mixed, high, low, sem):
        step = pl.program_id(0)
        steps = pl.num_programs(0)
        positions = sign_ref.shape[0]
        columns = x_ref.shape[1]

        @pl.when(step == 0)
        def _():
            me = me_ref[0]
            for device in range(devices):
                filled[device] = 0

            def place(p, state):
                owner, end = state
                owner, end = lax.while_loop(
                    lambda s: p >= s[1],
                    lambda s: (s[0] + 1, s[1] + counts_ref[0, s[0] + 1]),
                    (owner, end),
                )
                block = order_ref[0, p] - me * blocks_dev

                @pl.when((block >= 0) & (block < blocks_dev))
                def _():
                    slot = filled[owner]
                    filled[owner] = slot + 1
                    places[block] = p
                    targets[block] = lax.bitwise_xor(owner, me) * capacity + slot

                return owner, end

            lax.fori_loop(0, positions, place, (jnp.int32(0), counts_ref[0, 0]))
            masks = jnp.concatenate(
                [mask_ref[pl.ds(places[b], 1), :] for b in range(blocks_dev)], axis=0
            )
            signs = jnp.concatenate(
                [sign_ref[pl.ds(places[b], 1), :] for b in range(blocks_dev)], axis=0
            )
            upper = (iota((BLOCK, BLOCK), 0) <= iota((BLOCK, BLOCK), 1)).astype(bf16)
            running = dg(masks.astype(f32).astype(bf16), upper)
            ranked = jnp.where(masks == 1, running, 0.0)
            common = iota((BLOCK, BLOCK), 0) & iota((BLOCK, BLOCK), 1)
            for shift_by in (4, 2, 1):
                common = common ^ (common >> shift_by)
            walsh = (1 - 2 * (common & 1)).astype(f32).astype(bf16)
            rank = (iota((KEEP, BLOCK), 0) + 1).astype(f32)
            select = jnp.concatenate(
                [(ranked[b : b + 1, :] == rank).astype(f32) for b in range(blocks_dev)], axis=0
            )
            kept = dg(select.astype(bf16), walsh)
            flips = (1 - 2 * signs).astype(f32)
            for b in range(blocks_dev):
                transform[b * KEEP : (b + 1) * KEEP, :] = (
                    kept[b * KEEP : (b + 1) * KEEP, :] * flips[b : b + 1, :]
                ).astype(bf16)

        for half in range(STEP):
            row = pl.multiple_of((step * STEP + half) * KEEP, KEEP)
            t = transform[pl.ds(row, KEEP), :]
            xh, xl = split(x_ref[half * BLOCK : (half + 1) * BLOCK, :])
            s = (dg(t, xh) + dg(t, xl)) * (float(BLOCK) ** -0.5)
            mixed[pl.ds(row, KEEP), :] = s
            sh, sl = split(s)
            high[pl.ds(row, KEEP), :] = sh
            low[pl.ds(row, KEEP), :] = sl
            pltpu.make_async_copy(
                mixed.at[pl.ds(row, KEEP), :], slots_ref.at[targets[step * STEP + half]], sem
            ).start()

        @pl.when(step == steps - 1)
        def _():
            at = 0
            for i in range(columns // PB):
                rows = slice(i * PB, (i + 1) * PB)
                a = (high[:, rows], low[:, rows])
                b = (high[:, i * PB :], low[:, i * PB :])
                g = dot3(a, b, 0, 0) * scale
                for j in range(columns // PB - i):
                    gram_ref[at : at + PB, :] = g[:, j * PB : (j + 1) * PB]
                    at += PB
            for b in range(blocks_dev):
                pltpu.make_async_copy(
                    mixed.at[0:KEEP, :], slots_ref.at[0], sem
                ).wait()

    return kernel


def mix(me, order, counts, signs, masks, matrix, devices, capacity):
    blocks_dev = matrix.shape[0] // BLOCK
    columns = matrix.shape[1]
    positions = signs.shape[0]
    panels = columns // PB
    packed = panels * (panels + 1) // 2 * PB
    smem = pl.BlockSpec(memory_space=pltpu.SMEM)
    whole = pl.BlockSpec((positions, BLOCK), lambda i: (0, 0))
    return pl.pallas_call(
        mix_kernel(blocks_dev, devices, capacity, 1.0 / float(positions * KEEP)),
        grid=(blocks_dev // STEP,),
        in_specs=[smem, smem, smem, whole, whole,
                  pl.BlockSpec((STEP * BLOCK, columns), lambda i: (i, 0))],
        out_specs=[pl.BlockSpec(memory_space=pl.ANY),
                   pl.BlockSpec((packed, PB), lambda i: (0, 0))],
        out_shape=[jax.ShapeDtypeStruct((devices * capacity, KEEP, columns), f32),
                   jax.ShapeDtypeStruct((packed, PB), f32)],
        scratch_shapes=[
            pltpu.SMEM((blocks_dev,), jnp.int32),
            pltpu.SMEM((blocks_dev,), jnp.int32),
            pltpu.SMEM((devices,), jnp.int32),
            pltpu.VMEM((blocks_dev * KEEP, BLOCK), bf16),
            pltpu.VMEM((blocks_dev * KEEP, columns), f32),
            pltpu.VMEM((blocks_dev * KEEP, columns), bf16),
            pltpu.VMEM((blocks_dev * KEEP, columns), bf16),
            pltpu.SemaphoreType.DMA,
        ],
        name="mix_gram",
    )(me, order, counts, signs, masks, matrix)


def assemble_kernel(blocks_dev, devices, capacity, most):
    def kernel(me_ref, order_ref, counts_ref, *refs):
        arrived = refs[:devices]
        out_ref, zeros, filled, sem = refs[devices:]
        me = me_ref[0]
        zeros[...] = jnp.zeros_like(zeros)
        offset = jnp.int32(0)
        for device in range(devices):
            filled[device] = 0
            offset = offset + jnp.where(device < me, counts_ref[0, device], 0)
        count = counts_ref[0, me]

        def fill(j, carry):
            @pl.when(j < count)
            def _():
                source = order_ref[0, jnp.minimum(offset + j, order_ref.shape[1] - 1)] // blocks_dev
                slot = filled[source]
                filled[source] = slot + 1
                shift = lax.bitwise_xor(source, me)
                for s in range(devices):
                    @pl.when(shift == s)
                    def _():
                        pltpu.make_async_copy(arrived[s].at[slot], out_ref.at[j], sem).start()

            @pl.when(j >= count)
            def _():
                pltpu.make_async_copy(zeros, out_ref.at[j], sem).start()

            return carry

        lax.fori_loop(0, most, fill, 0)

        def drain(j, carry):
            pltpu.make_async_copy(zeros, out_ref.at[j], sem).wait()
            return carry

        lax.fori_loop(0, most, drain, 0)

    return kernel


def assemble(me, order, counts, arrived, blocks_dev, capacity, most):
    devices = len(arrived)
    columns = arrived[0].shape[-1]
    smem = pl.BlockSpec(memory_space=pltpu.SMEM)
    anywhere = pl.BlockSpec(memory_space=pl.ANY)
    return pl.pallas_call(
        assemble_kernel(blocks_dev, devices, capacity, most),
        in_specs=[smem, smem, smem] + [anywhere] * devices,
        out_specs=anywhere,
        out_shape=jax.ShapeDtypeStruct((most, KEEP, columns), f32),
        scratch_shapes=[pltpu.VMEM((KEEP, columns), f32),
                        pltpu.SMEM((devices,), jnp.int32),
                        pltpu.SemaphoreType.DMA],
        name="assemble",
    )(me, order, counts, *arrived)


def chain(R, C, lanes, store):
    inverse = jnp.zeros((BS, PB), f32)
    for k in range(BS):
        pivot = C[k][k : k + 1, :]
        reciprocal = 1.0 / pivot
        others = jnp.where(lanes == k, 0.0, C[k])
        ck = others * reciprocal
        for j in range(k + 1, BS):
            if j == k + 1:
                C[j] = C[j] - (others * C[j][k : k + 1, :]) * reciprocal
            else:
                C[j] = C[j] - ck * C[j][k : k + 1, :]
        root = lax.rsqrt(pivot)
        for t in range(len(R)):
            row = R[t][k : k + 1, :]
            store(t, k, row * root)
            R[t] = R[t] - ck * row
        inverse = jnp.where(lanes == k, reciprocal, inverse)
    return [r * inverse for r in R]


def factor_in_place(A, U, Ds, Gs, Us, Ws, n):
    panels = n // PB
    inner = PB // BS
    lanes = iota((BS, PB), 0)
    eye = (iota((PB, PB), 0) == iota((PB, PB), 1)).astype(f32)
    keep = iota((PB, PB), 1) >= iota((PB, PB), 0)
    row_n = iota((PB, n), 0)
    lane_n = iota((PB, n), 1)
    Ds[...] = A[0:PB, 0:PB]

    def body(panel, first):
        c0 = pl.multiple_of(panel * PB, PB)
        if not first:
            p0 = pl.multiple_of((panel - 1) * PB, PB)
            urow = dot3(split(Ws[...]), split(A[pl.ds(p0, PB), :]))
            urow = jnp.where(lane_n >= row_n + p0, urow, 0.0)
            U[pl.ds(p0, PB), :] = urow
            U[pl.ds(p0, PB), pl.ds(p0, PB)] = Us[...]
            uf = split(urow)
        Gs[...] = eye
        R = [Ds[0:BS, :], Gs[0:BS, :]]
        for m in range(inner):
            r0 = m * BS
            C = [jnp.broadcast_to(R[0][:, r0 + j : r0 + j + 1], (BS, PB)) for j in range(BS)]
            if m < inner - 1:
                An = [Ds[r0 + BS : r0 + 2 * BS, :], Gs[r0 + BS : r0 + 2 * BS, :]]
                Ln = [jnp.broadcast_to(An[0][:, r0 + j : r0 + j + 1], (BS, PB)) for j in range(BS)]

            def store(t, k, v):
                (Us if t == 0 else Ws)[r0 + k : r0 + k + 1, :] = v

            Z = chain(R, C, lanes, store)
            if m < inner - 1:
                following = []
                for t in range(2):
                    acc = [None] * 4
                    for k in range(BS):
                        p = Ln[k] * Z[t][k : k + 1, :]
                        acc[k % 4] = p if acc[k % 4] is None else acc[k % 4] + p
                    following.append(An[t] - ((acc[0] + acc[1]) + (acc[2] + acc[3])))
                rr = r0 + 2 * BS
                if rr < PB:
                    zh, zl = split(jnp.concatenate(Z, axis=1))

                    def pad(z):
                        parts = [z, jnp.zeros((PB - (m + 1) * BS, 2 * PB), bf16)]
                        if m:
                            parts = [jnp.zeros((m * BS, 2 * PB), bf16)] + parts
                        return jnp.concatenate(parts, axis=0)

                    update = dot3(split(Ds[rr:PB, :]), (pad(zh), pad(zl)))
                    Ds[rr:PB, :] = Ds[rr:PB, :] - update[:, :PB]
                    Gs[rr:PB, :] = Gs[rr:PB, :] - update[:, PB:]
                R = following
            if not first and 0 < m < panels:
                s = m * PB
                a = (uf[0][:, s : s + PB], uf[1][:, s : s + PB])
                b = (uf[0][:, s:], uf[1][:, s:])
                A[s : s + PB, s:] = A[s : s + PB, s:] - dot3(a, b, 0, 0)
        Us[...] = jnp.where(keep, Us[...], 0.0)
        nx = pl.multiple_of(jnp.minimum(panel + 1, panels - 1) * PB, PB)
        un = split(dot3(split(Ws[...]), split(A[pl.ds(c0, PB), pl.ds(nx, PB)])))
        Ds[...] = A[pl.ds(nx, PB), pl.ds(nx, PB)] - dot3(un, un, 0, 0)

    body(jnp.int32(0), True)

    def loop(panel, carry):
        body(panel, False)
        return carry

    lax.fori_loop(1, panels, loop, 0)
    U[n - PB : n, 0 : n - PB] = jnp.zeros((PB, n - PB), f32)
    U[n - PB : n, n - PB : n] = Us[...]


def factor_kernel(n, devices):
    panels = n // PB
    rows_dev = n // devices

    def kernel(me_ref, ga, gb, ma, mb, out_ref, A, U, Ds, Gs, Us, Ws, sem):
        me = me_ref[0]
        half = ga.shape[0]

        def load(first, second):
            at = 0
            for i in range(panels):
                for j in range(i, panels):
                    lo, hi = at, at + PB
                    at = hi
                    for src, base in ((first, 0), (second, half)):
                        s, e = max(lo, base), min(hi, base + half)
                        if s < e:
                            pltpu.make_async_copy(
                                src.at[s - base : e - base, :],
                                A.at[i * PB + s - lo : i * PB + e - lo, j * PB : (j + 1) * PB],
                                sem,
                            ).start()

        @pl.when(me % 2 == 0)
        def _():
            load(ga, gb)

        @pl.when(me % 2 == 1)
        def _():
            load(ma, mb)

        for i in range(panels):
            if i:
                A[i * PB : (i + 1) * PB, 0 : i * PB] = jnp.zeros((PB, i * PB), f32)
        for i in range(panels):
            for j in range(i, panels):
                pltpu.make_async_copy(
                    ga.at[0:PB, :], A.at[i * PB : (i + 1) * PB, j * PB : (j + 1) * PB], sem
                ).wait()
        factor_in_place(A, U, Ds, Gs, Us, Ws, n)
        mine = pl.multiple_of(me * rows_dev, rows_dev)
        other = pl.multiple_of(lax.bitwise_xor(me, 1) * rows_dev, rows_dev)
        first = pltpu.make_async_copy(U.at[pl.ds(mine, rows_dev), :], out_ref.at[0], sem)
        second = pltpu.make_async_copy(U.at[pl.ds(other, rows_dev), :], out_ref.at[1], sem)
        first.start()
        second.start()
        first.wait()
        second.wait()

    return kernel


def cholesky_rows(me, ga, gb, ma, mb, n, devices):
    rows_dev = n // devices
    smem = pl.BlockSpec(memory_space=pltpu.SMEM)
    anywhere = pl.BlockSpec(memory_space=pl.ANY)
    return pl.pallas_call(
        factor_kernel(n, devices),
        in_specs=[smem] + [anywhere] * 4,
        out_specs=anywhere,
        out_shape=jax.ShapeDtypeStruct((2, rows_dev, n), f32),
        scratch_shapes=[pltpu.VMEM((n, n), f32), pltpu.VMEM((n, n), f32)]
        + [pltpu.VMEM((PB, PB), f32)] * 4
        + [pltpu.SemaphoreType.DMA],
        name="cholesky",
    )(me, ga, gb, ma, mb)


def exchange_sum(x, axis, perm, bit):
    rows = x.shape[0] // 2
    low, high = x[:rows], x[rows:]
    arrived = lax.ppermute(jnp.where(bit == 0, high, low), axis, perm)
    return jnp.where(bit == 0, low, high) + arrived


def exchange_join(x, axis, perm, bit):
    arrived = lax.ppermute(x, axis, perm)
    return jnp.concatenate([jnp.where(bit == 0, x, arrived), jnp.where(bit == 0, arrived, x)], axis=0)


def body(matrix, block_order, counts, sign_bits, row_mask):
    blocks_dev = matrix.shape[0] // BLOCK
    columns = matrix.shape[1]
    devices = lax.axis_size("dev")
    groups = lax.axis_size("grp")
    me = lax.axis_index("dev").astype(jnp.int32)
    grp = lax.axis_index("grp").astype(jnp.int32)
    most = 2 * blocks_dev
    capacity = max(1, most // devices)
    core = me & 1
    me_array = me.reshape(1)

    slots, gram = mix(me_array, block_order, counts, sign_bits[0], row_mask[0], matrix, devices, capacity)
    pair = [(d, d ^ 1) for d in range(devices)]

    gram = exchange_sum(gram, "dev", pair, core)
    bits = [b for b in range(1, devices.bit_length() - 1)]
    orders = list(zip(bits, reversed(bits)))
    perms = [[(d, d ^ (1 << (o[d & 1]))) for d in range(devices)] for o in orders]
    mine = [jnp.where(core == 0, (me >> o[0]) & 1, (me >> o[1]) & 1) for o in orders]
    for perm, bit in zip(perms, mine):
        gram = exchange_sum(gram, "dev", perm, bit)

    def gather(x):
        for perm, bit in reversed(list(zip(perms, mine))):
            x = exchange_join(x, "dev", perm, bit)
        return x

    mean = gram * (1.0 / float(groups))
    levels = range(groups.bit_length() - 1)
    for b in levels:
        mean = exchange_sum(mean, "grp", [(g, g ^ (1 << b)) for g in range(groups)], (grp >> b) & 1)
    for b in reversed(levels):
        mean = exchange_join(mean, "grp", [(g, g ^ (1 << b)) for g in range(groups)], (grp >> b) & 1)

    group_half = gather(gram)
    group_other = lax.ppermute(group_half, "dev", [(d, d ^ 1) for d in range(devices) if d & 1])
    mean_half = gather(mean)
    mean_other = lax.ppermute(mean_half, "dev", [(d, d ^ 1) for d in range(devices) if not d & 1])
    rows = cholesky_rows(me_array, group_half, group_other, mean_other, mean_half, columns, devices)
    theirs = lax.ppermute(rows[1], "dev", pair)
    group_factor = jnp.where(core == 0, rows[0], theirs)[None]
    factor = jnp.where(core == 0, theirs, rows[0])

    slots, _ = lax.optimization_barrier((slots, mean_half[0:8]))
    slots = slots.reshape(devices, capacity, KEEP, columns)
    arrived = [slots[0]] + [
        lax.ppermute(slots[s], "dev", [(d, d ^ s) for d in range(devices)]) for s in range(1, devices)
    ]
    sketch = assemble(me_array, block_order, counts, arrived, blocks_dev, capacity, most)
    return (sketch.reshape(most * KEEP, columns), group_factor, factor)


def solution(mesh):
    placed = (
        P(("grp", "dev"), None),
        P("grp", None),
        P("grp", None),
        P("grp", None, None),
        P("grp", None, None),
    )
    return jax.shard_map(
        body,
        mesh=mesh,
        in_specs=placed,
        out_specs=(P(("grp", "dev"), None), P("grp", "dev", None), P("dev", None)),
        check_vma=False,
    )
```

time: 611 us -> 277 us (0.45)
  other arithmetic: 379 us -> 5.27 us
  Pallas kernels: 0 us -> 167 us
  matrix products: 61.8 us -> 0 us
  local copies, waits for them, and re-layouts: 36.9 us -> 6.63 us
  between operations: 25.1 us -> 0.92 us
  waiting for transfers between devices: 93.1 us -> 74.3 us
  starting transfers between devices: 5.48 us -> 17.5 us
    another operation x64 -> x0, other arithmetic: 346 us -> none  [the longest x31 173 us: body(): mean_upper = jnp.linalg.cholesky(mean_gram).T]
    pallas_call x0 -> x3, Pallas kernels: none -> 167 us  [the longest x1 125 us: assemble(): pl.pallas_call(assemble_kernel(blocks_dev, devices, capacity, most), in_s...]
    psum x2 -> x0, waiting for transfers between devices: 92.8 us -> none  [the longest x1 92.8 us: body(): group_gram = lax.psum(partial_value, 'dev') / float(positions * KEEP)]
    ppermute x0 -> x21, waiting for transfers between devices: none -> 74.3 us  [the longest x5 29.4 us: exchange_sum(): arrived = lax.ppermute(jnp.where(bit == 0, high, low), axis, perm)]
    another operation x28 -> x0, matrix products: 46.3 us -> none  [the longest x14 23.2 us: body(): group_upper = jnp.linalg.cholesky(group_gram).T]
    div x4 -> x0, other arithmetic: 18.9 us -> none  [the longest x1 5 us: body(): mean_gram = lax.psum(group_gram, 'grp') / float(groups)]
    ppermute x0 -> x21, starting transfers between devices: none -> 17.5 us  [the longest x7 6.31 us: body(): lax.ppermute(slots[s], 'dev', [(d, d ^ s) for d in range(devices)])]
    dot_general x3 -> x0, matrix products: 15.5 us -> none  [the longest x1 8.38 us: gram_of(): jnp.einsum('kc,ke->ce', flat_rows, flat_rows, precision=lax.Precision.HIG...]
  transfers between devices with their start and end apart: 3 -> 21, of which waited for: 1 -> 13; matrix products, arithmetic and copies ran while one was open for 39% -> 2% of each run, Pallas kernels for 0% -> 57%
where the time goes in v1:
time: 277 us; the launch traced here: 271 us
  Pallas kernels  167 us (60%)
  waiting for transfers between devices  74.3 us (27%)
  starting transfers between devices  17.5 us (6%)
  local copies, waits for them, and re-layouts  6.63 us (2%)
  other arithmetic  5.27 us (2%)
    pallas_call x1, Pallas kernels, assemble(): pl.pallas_call(assemble_kernel(blocks_dev, devices, capacity, most), in_s...  125 us
    ppermute x5, waiting for transfers between devices, exchange_sum(): arrived = lax.ppermute(jnp.where(bit == 0, high, low), axis, perm)  29.4 us
    pallas_call x1, Pallas kernels, cholesky_rows(): pl.pallas_call(factor_kernel(n, devices), in_specs=[smem] + [anywhere] *...  28.4 us
    ppermute x6, waiting for transfers between devices, exchange_join(): arrived = lax.ppermute(x, axis, perm)  24.3 us
    ppermute x7, waiting for transfers between devices, body(): lax.ppermute(slots[s], 'dev', [(d, d ^ s) for d in range(devices)])  20.6 us
    pallas_call x1, Pallas kernels, mix(): pl.pallas_call(mix_kernel(blocks_dev, devices, capacity, 1.0 / float(posi...  13.4 us
    ppermute x7, starting transfers between devices, body(): lax.ppermute(slots[s], 'dev', [(d, d ^ s) for d in range(devices)])  6.31 us
  transfers between devices with their start and end apart: 21, of which 13 were waited for; matrix products, arithmetic and copies ran while one was open for 2% of the time, Pallas kernels for 57%

profile of v1, /device:TPU:26, one launch (start us, length us, event | category | flops | bytes accessed | tf_op | source)
XLA Modules:
  0.0 271.4 jit_solution(3311763293172202378)
XLA Ops:
  0.6 13.4 %mix_gram.1 = (f32[32,32,1024]{2,1,0:T(8,128)}, f32[4608,128]{1,0:T(8,128)}) custom-call(s32[1]{0:T(128)} %bitcast.me_ref, s32[1,128]{1,0:T(1,128)} %order_ref.3, s32[1,8]{1,0:T(1,128)} %counts_ref.3, s32[128,128]{1,0:T(8,128)} %bitcast.15, s32[128,128]{1,0:T(8,128)} %bitcast.16, f32[2048,1024]{1,0:T(8,128)} %x_ref.1), custom_call_target="tpu_custom_call" | custom-call | tf_op jit(solution)/shard_map/mix_gram/pallas_call | solution.py:131
  14.1 1.9 slice_select_fusion
  16.1 3.0 %collective-permute-done.7 = f32[2304,128]{1,0:T(8,128)} collective-permute-done((f32[2304,128]{1,0:T(8,128)S(1)}, f32[2304,128]{1,0:T(8,128)}, u32[]{:S(2)}, u32[]{:S(2)}) %collective-permute-start.7) | collective-permute-done | bytes 1179680 | tf_op jit(solution)/shard_map/ppermute | solution.py:379
  19.0 1.4 select_add_fusion
  21.1 9.3 %collective-permute-done.8 = f32[1152,128]{1,0:T(8,128)S(1)} collective-permute-done((f32[1152,128]{1,0:T(8,128)S(1)}, f32[1152,128]{1,0:T(8,128)S(1)}, u32[]{:S(2)}, u32[]{:S(2)}) %collective-permute-start.8) | collective-permute-done | bytes 589856 | tf_op jit(solution)/shard_map/ppermute | solution.py:379
  30.6 1.6 collective-permute-start.9
  32.2 5.2 %collective-permute-done.9 = f32[576,128]{1,0:T(8,128)S(1)} collective-permute-done((f32[576,128]{1,0:T(8,128)S(1)}, f32[576,128]{1,0:T(8,128)S(1)}, u32[]{:S(2)}, u32[]{:S(2)}) %collective-permute-start.9) | collective-permute-done | bytes 294944 | tf_op jit(solution)/shard_map/ppermute | solution.py:379
  38.0 4.7 %collective-permute-done.13 = f32[288,128]{1,0:T(8,128)S(1)} collective-permute-done((f32[288,128]{1,0:T(8,128)S(1)}, f32[288,128]{1,0:T(8,128)S(1)}, u32[]{:S(2)}, u32[]{:S(2)}) %collective-permute-start.13) | collective-permute-done | bytes 147488 | tf_op jit(solution)/shard_map/ppermute | solution.py:379
  43.1 7.2 %collective-permute-done.14 = f32[144,128]{1,0:T(8,128)S(1)} collective-permute-done((f32[144,128]{1,0:T(8,128)S(1)}, f32[144,128]{1,0:T(8,128)S(1)}, u32[]{:S(2)}, u32[]{:S(2)}) %collective-permute-start.14) | collective-permute-done | bytes 73760 | tf_op jit(solution)/shard_map/ppermute | solution.py:379
  50.4 1.6 collective-permute-start.10
  52.0 3.6 %collective-permute-done.15 = f32[144,128]{1,0:T(8,128)S(1)} collective-permute-done((f32[144,128]{1,0:T(8,128)S(1)}, f32[144,128]{1,0:T(8,128)S(1)}, u32[]{:S(2)}, u32[]{:S(2)}) %collective-permute-start.15) | collective-permute-done | bytes 73760 | tf_op jit(solution)/shard_map/ppermute | solution.py:384
  55.8 1.4 collective-permute-done.10
  57.3 3.6 %collective-permute-done.16 = f32[288,128]{1,0:T(8,128)S(1)} collective-permute-done((f32[288,128]{1,0:T(8,128)S(1)}, f32[288,128]{1,0:T(8,128)S(1)}, u32[]{:S(2)}, u32[]{:S(2)}) %collective-permute-start.16) | collective-permute-done | bytes 147488 | tf_op jit(solution)/shard_map/ppermute | solution.py:384
  60.9 1.6 collective-permute-start.17
  63.2 7.7 %collective-permute-done.17 = f32[576,128]{1,0:T(8,128)S(1)} collective-permute-done((f32[576,128]{1,0:T(8,128)S(1)}, f32[576,128]{1,0:T(8,128)S(1)}, u32[]{:S(2)}, u32[]{:S(2)}) %collective-permute-start.17) | collective-permute-done | bytes 294944 | tf_op jit(solution)/shard_map/ppermute | solution.py:384
  71.6 0.9 collective-permute-done.11
  72.7 1.3 collective-permute-start.12
  74.0 6.9 %collective-permute-done.18 = f32[1152,128]{1,0:T(8,128)S(1)} collective-permute-done((f32[1152,128]{1,0:T(8,128)S(1)}, f32[1152,128]{1,0:T(8,128)S(1)}, u32[]{:S(2)}, u32[]{:S(2)}) %collective-permute-start.18) | collective-permute-done | bytes 589856 | tf_op jit(solution)/shard_map/ppermute | solution.py:384
  81.1 1.6 collective-permute-start.19
  83.5 2.1 fusion.1
  86.2 1.2 collective-permute-start.2
  87.5 1.5 collective-permute-start.3
  89.0 1.0 copy-done.6
  90.4 28.4 %cholesky.1 = f32[2,128,1024]{2,1,0:T(8,128)} custom-call(s32[1]{0:T(128)} %bitcast.me_ref, f32[2304,128]{1,0:T(8,128)} %copy-done.1, f32[2304,128]{1,0:T(8,128)} %copy-done.5, f32[2304,128]{1,0:T(8,128)} %copy-done.6, f32[2304,128]{1,0:T(8,128)} %copy-done.2), custom_call_target="tpu_custom_call" | custom-call | tf_op jit(solution)/shard_map/cholesky/pallas_call | solution.py:364
  118.8 1.4 collective-permute-start.5
  120.2 1.2 collective-permute-start.6
  121.4 1.9 slice_bitcast_fusion
  123.8 10.8 %collective-permute-done.5.refs_6_ = f32[4,32,1024]{2,1,0:T(8,128)S(1)} collective-permute-done((f32[4,32,1024]{2,1,0:T(8,128)S(1)}, f32[4,32,1024]{2,1,0:T(8,128)S(1)}, u32[]{:S(2)}, u32[]{:S(2)}) %collective-permute-start.5) | collective-permute-done | bytes 524320 | tf_op jit(solution)/shard_map/ppermute | solution.py:435
  134.6 9.9 %collective-permute-done.6.refs_7_ = f32[4,32,1024]{2,1,0:T(8,128)S(1)} collective-permute-done((f32[4,32,1024]{2,1,0:T(8,128)S(1)}, f32[4,32,1024]{2,1,0:T(8,128)S(1)}, u32[]{:S(2)}, u32[]{:S(2)}) %collective-permute-start.6) | collective-permute-done | bytes 524320 | tf_op jit(solution)/shard_map/ppermute | solution.py:435
  144.4 0.8 copy-done.11
  145.3 125.0 %assemble.1 = f32[32,32,1024]{2,1,0:T(8,128)} custom-call(s32[1]{0:T(128)} %bitcast.me_ref, s32[1,128]{1,0:T(1,128)} %order_ref.3, s32[1,8]{1,0:T(1,128)} %counts_ref.3, f32[4,32,1024]{2,1,0:T(8,128)} %get-tuple-element.16.refs_0_, f32[4,32,1024]{2,1,0:T(8,128)} %collective-permute-done.refs_1_, f32[4,32,1024]{2,1,0:T(8,128)} %collective-permute-done.1.refs_2_, ...), custom_call_target="tpu_custom_call" | custom-call | tf_op jit(solution)/shard_map/assemble/pallas_call | solution.py:200
  270.3 1.0 fusion
  (62 shorter events, 6.1 us)
Async XLA Ops:
  14.1 5.0 %copy-start = (f32[4608,128]{1,0:T(8,128)S(1)}, f32[4608,128]{1,0:T(8,128)}, u32[]{:S(2)}) copy-start(f32[4608,128]{1,0:T(8,128)} %get-tuple-element.6) | copy-start | bytes 7077892
  16.0 3.0 %collective-permute-start.7 = (f32[2304,128]{1,0:T(8,128)S(1)}, f32[2304,128]{1,0:T(8,128)}, u32[]{:S(2)}, u32[]{:S(2)}) collective-permute-start(f32[2304,128]{1,0:T(8,128)S(1)} %slice_select_fusion), channel_id=1, source_target_pairs={{0,1},{1,0},{2,3},{3,2},{4,5},{5,4},{6,7},{7,6},{8,9},{9,8},{10,11... | collective-permute-start | bytes 3538952 | tf_op jit(solution)/shard_map/ppermute | solution.py:379
  20.5 9.9 %collective-permute-start.8 = (f32[1152,128]{1,0:T(8,128)S(1)}, f32[1152,128]{1,0:T(8,128)S(1)}, u32[]{:S(2)}, u32[]{:S(2)}) collective-permute-start(f32[1152,128]{1,0:T(8,128)S(1)} %slice_select_fusion.1), channel_id=1, source_target_pairs={{0,2},{1,5},{2,0},{3,7},{4,6},{5,1},{6,4},{7,3},{8,10},{9,13},{10,... | collective-permute-start | bytes 1769480 | tf_op jit(solution)/shard_map/ppermute | solution.py:379
  30.6 6.8 %collective-permute-start.9 = (f32[576,128]{1,0:T(8,128)S(1)}, f32[576,128]{1,0:T(8,128)S(1)}, u32[]{:S(2)}, u32[]{:S(2)}) collective-permute-start(f32[576,128]{1,0:T(8,128)S(1)} %slice_select_fusion.2), channel_id=1, source_target_pairs={{0,4},{1,3},{2,6},{3,1},{4,0},{5,7},{6,2},{7,5},{8,12},{9,11},{10,... | collective-permute-start | bytes 884744 | tf_op jit(solution)/shard_map/ppermute | solution.py:379
  37.5 5.2 %collective-permute-start.13 = (f32[288,128]{1,0:T(8,128)S(1)}, f32[288,128]{1,0:T(8,128)S(1)}, u32[]{:S(2)}, u32[]{:S(2)}) collective-permute-start(f32[288,128]{1,0:T(8,128)S(1)} %slice_select_fusion.3), channel_id=1, source_target_pairs={{0,8},{8,0},{16,24},{24,16},{1,9},{9,1},{17,25},{25,17},{2,10},{10... | collective-permute-start | bytes 442376 | tf_op jit(solution)/shard_map/ppermute | solution.py:379
  42.7 7.6 %collective-permute-start.14 = (f32[144,128]{1,0:T(8,128)S(1)}, f32[144,128]{1,0:T(8,128)S(1)}, u32[]{:S(2)}, u32[]{:S(2)}) collective-permute-start(f32[144,128]{1,0:T(8,128)S(1)} %slice_select_fusion.4), channel_id=1, source_target_pairs={{0,16},{8,24},{16,0},{24,8},{1,17},{9,25},{17,1},{25,9},{2,18},{10... | collective-permute-start | bytes 221192 | tf_op jit(solution)/shard_map/ppermute | solution.py:379
  50.3 5.3 %collective-permute-start.15 = (f32[144,128]{1,0:T(8,128)S(1)}, f32[144,128]{1,0:T(8,128)S(1)}, u32[]{:S(2)}, u32[]{:S(2)}) collective-permute-start(f32[144,128]{1,0:T(8,128)S(1)} %select_add_fusion.4), channel_id=1, source_target_pairs={{0,16},{8,24},{16,0},{24,8},{1,17},{9,25},{17,1},{25,9},{2,18},{10... | collective-permute-start | bytes 221192 | tf_op jit(solution)/shard_map/ppermute | solution.py:384
  50.4 6.8 %collective-permute-start.10 = (f32[576,128]{1,0:T(8,128)S(1)}, f32[576,128]{1,0:T(8,128)S(1)}, u32[]{:S(2)}, u32[]{:S(2)}) collective-permute-start(f32[576,128]{1,0:T(8,128)S(1)} %get-tuple-element.8), channel_id=1, source_target_pairs={{0,4},{1,3},{2,6},{3,1},{4,0},{5,7},{6,2},{7,5},{8,12},{9,11},{10,... | collective-permute-start | bytes 884744 | tf_op jit(solution)/shard_map/ppermute | solution.py:384
  55.7 5.2 %collective-permute-start.16 = (f32[288,128]{1,0:T(8,128)S(1)}, f32[288,128]{1,0:T(8,128)S(1)}, u32[]{:S(2)}, u32[]{:S(2)}) collective-permute-start(f32[288,128]{1,0:T(8,128)S(1)} %pad_maximum_fusion.5), channel_id=1, source_target_pairs={{0,8},{8,0},{16,24},{24,16},{1,9},{9,1},{17,25},{25,17},{2,10},{10... | collective-permute-start | bytes 442376 | tf_op jit(solution)/shard_map/ppermute | solution.py:384
  60.9 9.9 %collective-permute-start.17 = (f32[576,128]{1,0:T(8,128)S(1)}, f32[576,128]{1,0:T(8,128)S(1)}, u32[]{:S(2)}, u32[]{:S(2)}) collective-permute-start(f32[576,128]{1,0:T(8,128)S(1)} %pad_maximum_fusion.4), channel_id=1, source_target_pairs={{0,4},{1,3},{2,6},{3,1},{4,0},{5,7},{6,2},{7,5},{8,12},{9,11},{10,... | collective-permute-start | bytes 884744 | tf_op jit(solution)/shard_map/ppermute | solution.py:384
  62.6 9.9 %collective-permute-start.11 = (f32[1152,128]{1,0:T(8,128)S(1)}, f32[1152,128]{1,0:T(8,128)S(1)}, u32[]{:S(2)}, u32[]{:S(2)}) collective-permute-start(f32[1152,128]{1,0:T(8,128)S(1)} %pad_maximum_fusion.2), channel_id=1, source_target_pairs={{0,2},{1,5},{2,0},{3,7},{4,6},{5,1},{6,4},{7,3},{8,10},{9,13},{10,... | collective-permute-start | bytes 1769480 | tf_op jit(solution)/shard_map/ppermute | solution.py:384
  71.0 9.9 %collective-permute-start.18 = (f32[1152,128]{1,0:T(8,128)S(1)}, f32[1152,128]{1,0:T(8,128)S(1)}, u32[]{:S(2)}, u32[]{:S(2)}) collective-permute-start(f32[1152,128]{1,0:T(8,128)S(1)} %pad_maximum_fusion.3), channel_id=1, source_target_pairs={{0,2},{1,5},{2,0},{3,7},{4,6},{5,1},{6,4},{7,3},{8,10},{9,13},{10,... | collective-permute-start | bytes 1769480 | tf_op jit(solution)/shard_map/ppermute | solution.py:384
  72.7 8.3 %copy-start.1 = (f32[2304,128]{1,0:T(8,128)}, f32[2304,128]{1,0:T(8,128)S(1)}, u32[]{:S(2)}) copy-start(f32[2304,128]{1,0:T(8,128)S(1)} %pad_maximum_fusion.ga) | copy-start | bytes 3538948
  72.7 14.8 %collective-permute-start.12 = (f32[2304,128]{1,0:T(8,128)S(1)}, f32[2304,128]{1,0:T(8,128)S(1)}, u32[]{:S(2)}, u32[]{:S(2)}) collective-permute-start(f32[2304,128]{1,0:T(8,128)S(1)} %pad_maximum_fusion.ga), channel_id=1, source_target_pairs={{1,0},{3,2},{5,4},{7,6},{9,8},{11,10},{13,12},{15,14},{17,16},{19,... | collective-permute-start | bytes 3538952 | tf_op jit(solution)/shard_map/ppermute | solution.py:424
  80.9 2.6 copy-start.3
  81.1 4.5 %copy-start.2 = (f32[2304,128]{1,0:T(8,128)}, f32[2304,128]{1,0:T(8,128)S(1)}, u32[]{:S(2)}) copy-start(f32[2304,128]{1,0:T(8,128)S(1)} %pad_maximum_fusion.1.mb) | copy-start | bytes 3538948
  81.1 7.9 %collective-permute-start.19 = (f32[2304,128]{1,0:T(8,128)S(1)}, f32[2304,128]{1,0:T(8,128)S(1)}, u32[]{:S(2)}, u32[]{:S(2)}) collective-permute-start(f32[2304,128]{1,0:T(8,128)S(1)} %pad_maximum_fusion.1.mb), channel_id=1, source_target_pairs={{0,1},{2,3},{4,5},{6,7},{8,9},{10,11},{12,13},{14,15},{16,17},{18,... | collective-permute-start | bytes 3538952 | tf_op jit(solution)/shard_map/ppermute | solution.py:426
  85.6 33.2 %collective-permute-start = (f32[4,32,1024]{2,1,0:T(8,128)}, f32[4,32,1024]{2,1,0:T(8,128)}, u32[]{:S(2)}, u32[]{:S(2)}) collective-permute-start(f32[4,32,1024]{2,1,0:T(8,128)} %get-tuple-element.15), channel_id=1, source_target_pairs={{0,1},{1,0},{2,3},{3,2},{4,5},{5,4},{6,7},{7,6},{8,9},{9,8},{10,11... | collective-permute-start | bytes 1572872 | tf_op jit(solution)/shard_map/ppermute | solution.py:435
  85.6 34.6 %collective-permute-start.1 = (f32[4,32,1024]{2,1,0:T(8,128)}, f32[4,32,1024]{2,1,0:T(8,128)}, u32[]{:S(2)}, u32[]{:S(2)}) collective-permute-start(f32[4,32,1024]{2,1,0:T(8,128)} %get-tuple-element.14), channel_id=1, source_target_pairs={{0,2},{1,3},{2,0},{3,1},{4,6},{5,7},{6,4},{7,5},{8,10},{9,11},{10,... | collective-permute-start | bytes 1572872 | tf_op jit(solution)/shard_map/ppermute | solution.py:435
  86.2 37.1 %collective-permute-start.2 = (f32[4,32,1024]{2,1,0:T(8,128)}, f32[4,32,1024]{2,1,0:T(8,128)}, u32[]{:S(2)}, u32[]{:S(2)}) collective-permute-start(f32[4,32,1024]{2,1,0:T(8,128)} %get-tuple-element.13), channel_id=1, source_target_pairs={{0,3},{1,2},{2,1},{3,0},{4,7},{5,6},{6,5},{7,4},{8,11},{9,10},{10,... | collective-permute-start | bytes 1572872 | tf_op jit(solution)/shard_map/ppermute | solution.py:435
  87.5 2.9 %copy-start.5 = (f32[2304,128]{1,0:T(8,128)}, f32[2304,128]{1,0:T(8,128)S(1)}, u32[]{:S(2)}) copy-start(f32[2304,128]{1,0:T(8,128)S(1)} %collective-permute-done.12.gb) | copy-start | bytes 3538948
  87.5 36.3 %collective-permute-start.3 = (f32[4,32,1024]{2,1,0:T(8,128)}, f32[4,32,1024]{2,1,0:T(8,128)}, u32[]{:S(2)}, u32[]{:S(2)}) collective-permute-start(f32[4,32,1024]{2,1,0:T(8,128)} %get-tuple-element.12), channel_id=1, source_target_pairs={{0,4},{1,5},{2,6},{3,7},{4,0},{5,1},{6,2},{7,3},{8,12},{9,13},{10,... | collective-permute-start | bytes 1572872 | tf_op jit(solution)/shard_map/ppermute | solution.py:435
  89.0 1.0 copy-start.6
  90.0 28.8 %copy-start.8 = (f32[4,32,1024]{2,1,0:T(8,128)S(1)}, f32[4,32,1024]{2,1,0:T(8,128)}, u32[]{:S(2)}) copy-start(f32[4,32,1024]{2,1,0:T(8,128)} %get-tuple-element.10) | copy-start | bytes 1572868
  90.0 30.2 %copy-start.7 = (f32[4,32,1024]{2,1,0:T(8,128)S(1)}, f32[4,32,1024]{2,1,0:T(8,128)}, u32[]{:S(2)}) copy-start(f32[4,32,1024]{2,1,0:T(8,128)} %get-tuple-element.9) | copy-start | bytes 1572868
  90.0 33.8 %collective-permute-start.4 = (f32[4,32,1024]{2,1,0:T(8,128)}, f32[4,32,1024]{2,1,0:T(8,128)S(1)}, u32[]{:S(2)}, u32[]{:S(2)}) collective-permute-start(f32[4,32,1024]{2,1,0:T(8,128)} %get-tuple-element.11), channel_id=1, source_target_pairs={{0,5},{1,4},{2,7},{3,6},{4,1},{5,0},{6,3},{7,2},{8,13},{9,12},{10,... | collective-permute-start | bytes 1572872 | tf_op jit(solution)/shard_map/ppermute | solution.py:435
  118.8 15.8 %collective-permute-start.5 = (f32[4,32,1024]{2,1,0:T(8,128)S(1)}, f32[4,32,1024]{2,1,0:T(8,128)S(1)}, u32[]{:S(2)}, u32[]{:S(2)}) collective-permute-start(f32[4,32,1024]{2,1,0:T(8,128)S(1)} %copy-done.8), channel_id=1, source_target_pairs={{0,6},{1,7},{2,4},{3,5},{4,2},{5,3},{6,0},{7,1},{8,14},{9,15},{10,... | collective-permute-start | bytes 1572872 | tf_op jit(solution)/shard_map/ppermute | solution.py:435
  120.2 24.2 %collective-permute-start.6 = (f32[4,32,1024]{2,1,0:T(8,128)S(1)}, f32[4,32,1024]{2,1,0:T(8,128)S(1)}, u32[]{:S(2)}, u32[]{:S(2)}) collective-permute-start(f32[4,32,1024]{2,1,0:T(8,128)S(1)} %copy-done.7), channel_id=1, source_target_pairs={{0,7},{1,6},{2,5},{3,4},{4,3},{5,2},{6,1},{7,0},{8,15},{9,14},{10,... | collective-permute-start | bytes 1572872 | tf_op jit(solution)/shard_map/ppermute | solution.py:435
  123.3 147.0 %collective-permute-start.20 = (f32[128,1024]{1,0:T(8,128)}, f32[128,1024]{1,0:T(8,128)S(1)}, u32[]{:S(2)}, u32[]{:S(2)}) collective-permute-start(f32[128,1024]{1,0:T(8,128)} %slice_bitcast_fusion), channel_id=1, source_target_pairs={{0,1},{1,0},{2,3},{3,2},{4,5},{5,4},{6,7},{7,6},{8,9},{9,8},{10,11... | collective-permute-start | bytes 1572872 | tf_op jit(solution)/shard_map/ppermute | solution.py:428
  123.8 20.6 %copy-start.9 = (f32[4,32,1024]{2,1,0:T(8,128)}, f32[4,32,1024]{2,1,0:T(8,128)S(1)}, u32[]{:S(2)}) copy-start(f32[4,32,1024]{2,1,0:T(8,128)S(1)} %collective-permute-done.4.refs_5_) | copy-start | bytes 1572868
  134.6 9.9 %copy-start.10 = (f32[4,32,1024]{2,1,0:T(8,128)}, f32[4,32,1024]{2,1,0:T(8,128)S(1)}, u32[]{:S(2)}) copy-start(f32[4,32,1024]{2,1,0:T(8,128)S(1)} %collective-permute-done.5.refs_6_) | copy-start | bytes 1572868
  145.3 125.1 %copy-start.4 = (f32[2,128,1024]{2,1,0:T(8,128)S(1)}, f32[2,128,1024]{2,1,0:T(8,128)}, u32[]{:S(2)}) copy-start(f32[2,128,1024]{2,1,0:T(8,128)} %cholesky.1) | copy-start | bytes 3145732
  (1 other events, 0.8 us)
